TPU v7x, 32 devices: a whole 2x2x4 slice. The times are simulated.
32 devices in a mesh: req: 8 (over z, y), tp: 4 (over x, core).
Axes of the slice: x: 2, y: 2, z: 4, core: 2. Of those that a mesh axis runs over, the one named last changes fastest.
Arguments:
- tokens: bfloat16 [16, 1024], P('req'), may hold values from -4 to 4
- slot_of: int32 [16], replicated, may hold values from 0 to 15, each once
- key_cache: bfloat16 [16, 1536, 1024], P('req', None, 'tp'), may hold values from -1100 to 1100
- value_cache: bfloat16 [16, 1536, 1024], P('req', None, 'tp'), may hold values from -6 to 6
- cache_len: int32 [16], P('req'), may hold values from 1 to 1536, as said below
- rel_bucket: int32 [16, 1536], P('req'), may hold values from 0 to 511
- rel_table: bfloat16 [512, 1024], P('req'), may hold values from -6 to 6
- w_query: bfloat16 [1024, 1024], P(None, 'tp'), may hold values from -0.1875 to 0.1875
- w_key: bfloat16 [1024, 1024], P(None, 'tp'), may hold values from -0.1875 to 0.1875
- w_out: bfloat16 [1024, 1024], P('tp'), may hold values from -0.1875 to 0.1875
- out_gain: float32 [1024], P('tp'), may hold values from 0.1 to 1.9
- out_bias: float32 [1024], P('tp'), may hold values from -0.5 to 0.5
Outputs:
- normed: bfloat16 [16, 1024], P('req', 'tp')
Inputs may be any that keep to these rules, and one draw needn't show every extreme that they name: slot_of names every slot exactly once. `cache_len`: some slot holds exactly 1536 live positions in every draw.
All inputs are finite; a program needn't handle non-finite values.
Results may differ from a plain program's by a relative error of at most 0.0034.
The roundings to bfloat16 on the way count: a program that leaves them out, or rounds other values in their place, can miss the bound.
Values may be sent and summed in bfloat16 or wider, within the bound.
No kernel may reach another device: no remote copies, remote signals or barrier semaphores. Data moves between devices by JAX's collectives and lax.ppermute only.
A program may use at most 64 MiB of HBM per device.

v0:
```python
import math
import jax
import jax.numpy as jnp
from jax import lax
from jax.sharding import PartitionSpec as P

HD = 64
BUCKETS = 512
MAXLEN = 1536
BLOCK = 512
epsilon = 1e-06
masked_score = -1e30


def norm_rows(matrix):
    row_mean = jnp.mean(matrix, axis=-1, keepdims=True)
    centred = matrix - row_mean
    variance = jnp.mean(centred * centred, axis=-1, keepdims=True)
    return centred * lax.rsqrt(variance + epsilon)


def project_rows(shard_rows, w_key, w_query):
    normed_rows = norm_rows(shard_rows.astype(jnp.float32)).astype(jnp.bfloat16)
    key_part = jnp.dot(normed_rows, w_key, preferred_element_type=jnp.float32).astype(jnp.bfloat16)
    query_part = jnp.dot(normed_rows, w_query, preferred_element_type=jnp.float32).astype(
        jnp.bfloat16
    )
    return jnp.concatenate((key_part, query_part), axis=1)


def block_scores(offset, key_rows, bucket_rows, query_heads, rel_key, rel_query):
    local_heads = query_heads.shape[0]
    block_keys = lax.dynamic_slice_in_dim(key_rows, offset, BLOCK, 0)
    forward = lax.dynamic_slice_in_dim(bucket_rows, offset, BLOCK, 0)
    backward = jnp.minimum(BUCKETS - forward, BUCKETS - 1)
    table_ids = jnp.arange(BUCKETS, dtype=jnp.int32)
    one_fwd = (forward[:, None] == table_ids[None, :]).astype(jnp.bfloat16)
    one_back = (backward[:, None] == table_ids[None, :]).astype(jnp.bfloat16)
    rows_fwd = jnp.dot(one_fwd, rel_key, preferred_element_type=jnp.float32).reshape(
        BLOCK, local_heads, HD
    )
    rows_back = jnp.dot(one_back, rel_query, preferred_element_type=jnp.float32).reshape(
        BLOCK, local_heads, HD
    )
    key_heads = block_keys.reshape(BLOCK, local_heads, HD)
    content = jnp.einsum("hd,jhd->hj", query_heads, key_heads, preferred_element_type=jnp.float32)
    along_key = jnp.einsum("hd,jhd->hj", query_heads.astype(jnp.float32), rows_fwd)
    against = jnp.sum(key_heads.astype(jnp.float32) * rows_back, axis=2).T
    return (content + along_key + against) * (1.0 / math.sqrt(3.0 * HD))


def attend_slot(query_own, key_rows, value_rows, bucket_rows, length, rel_key, rel_query):
    local_heads = query_own.shape[0] // HD
    query_heads = query_own.reshape(local_heads, HD)
    block_count = (length + BLOCK - 1) // BLOCK

    def block_step(block_index, buffer):
        offset = block_index * BLOCK
        block_part = block_scores(offset, key_rows, bucket_rows, query_heads, rel_key, rel_query)
        return lax.dynamic_update_slice_in_dim(buffer, block_part, offset, 1)

    scores = lax.fori_loop(
        0, block_count, block_step, jnp.full((local_heads, MAXLEN), masked_score, jnp.float32)
    )
    positions = jnp.arange(MAXLEN, dtype=jnp.int32)
    live_keys = (positions < length)[None, :]
    scores = jnp.where(live_keys, scores, masked_score)
    highest = jnp.max(scores, axis=1, keepdims=True)
    exponent = jnp.where(live_keys, jnp.exp(scores - highest), 0.0)
    weights = (exponent / jnp.sum(exponent, axis=1, keepdims=True)).astype(jnp.bfloat16)
    value_heads = value_rows.reshape(MAXLEN, local_heads, HD)
    context = jnp.einsum("hj,jhd->hd", weights, value_heads, preferred_element_type=jnp.float32)
    return context.reshape(local_heads * HD).astype(jnp.bfloat16)


def per_device(
    tokens,
    slot_of,
    key_cache,
    value_cache,
    cache_len,
    rel_bucket,
    rel_table,
    w_query,
    w_key,
    w_out,
    out_gain,
    out_bias,
):
    rows_dev = tokens.shape[0]
    col_width = w_query.shape[1]
    rel_both = project_rows(lax.all_gather(rel_table, "req", axis=0, tiled=True), w_key, w_query)
    rel_key = rel_both[:, :col_width]
    rel_query = rel_both[:, col_width:]
    queries = jnp.dot(tokens, w_query, preferred_element_type=jnp.float32).astype(jnp.bfloat16)
    all_queries = lax.all_gather(queries, "req", axis=0, tiled=True)
    first_row = lax.axis_index("req") * rows_dev
    own_rows = first_row + jnp.arange(rows_dev, dtype=jnp.int32)
    request_count = slot_of.shape[0]
    chooser = (slot_of[None, :] == own_rows[:, None]).astype(jnp.bfloat16)
    own_queries = jnp.dot(chooser, all_queries, preferred_element_type=jnp.float32).astype(
        jnp.bfloat16
    )
    contexts = []
    for slot_index in range(rows_dev):
        contexts.append(
            attend_slot(
                own_queries[slot_index],
                key_cache[slot_index],
                value_cache[slot_index],
                rel_bucket[slot_index],
                cache_len[slot_index],
                rel_key,
                rel_query,
            )
        )
    own_context = jnp.stack(contexts, axis=0)
    all_contexts = lax.all_gather(own_context, "req", axis=0, tiled=True)
    own_slots = lax.dynamic_slice_in_dim(slot_of, first_row, rows_dev, 0)
    picker = (own_slots[:, None] == jnp.arange(request_count, dtype=jnp.int32)[None, :]).astype(
        jnp.bfloat16
    )
    context_rows = jnp.dot(picker, all_contexts, preferred_element_type=jnp.float32).astype(
        jnp.bfloat16
    )
    partial_out = jnp.dot(context_rows, w_out, preferred_element_type=jnp.float32)
    col_start = lax.axis_index("tp") * col_width
    row_sum = lax.psum(partial_out, "tp")
    normed_full = norm_rows(row_sum + tokens.astype(jnp.float32))
    own_cols = lax.dynamic_slice_in_dim(normed_full, col_start, col_width, 1)
    return (own_cols * out_gain + out_bias).astype(jnp.bfloat16)


def solution(mesh):
    in_specs = (
        P("req", None),
        P(),
        P("req", None, "tp"),
        P("req", None, "tp"),
        P("req"),
        P("req", None),
        P("req", None),
        P(None, "tp"),
        P(None, "tp"),
        P("tp", None),
        P("tp"),
        P("tp"),
    )
    out_specs = P("req", "tp")
    return jax.shard_map(
        per_device, mesh=mesh, in_specs=in_specs, out_specs=out_specs, check_vma=False
    )
```

profile of v0, /device:TPU:0, one launch (start us, length us, event | category | flops | bytes accessed | tf_op | source)
XLA Modules:
  0.0 98.8 jit_solution(9995086282330034420)
XLA Ops:
  6.5 0.0 copy-start
  6.5 0.0 all-gather.4.cloned.1.call-start
  6.5 0.7 all-gather.4.cloned.1.call-update
  7.3 1.4 %fusion.53 = (s32[1]{0:T(128)}, s32[1]{0:T(128)}) fusion(s32[2]{0:T(128)} %param.20), kind=kLoop, calls=%fused_computation.89 | loop fusion | bytes 16 | tf_op jit(solution)/shard_map/slice | solution.py:112
  10.1 0.0 copy-done
  10.1 0.9 fusion.25
  10.9 22.3 %all-gather = bf16[8,2,256]{2,1,0:T(2,128)(2,1)S(1)} all-gather(bf16[1,2,256]{2,1,0:T(2,128)(2,1)S(1)} %fusion.25), channel_id=1, replica_groups=mesh['req'=8,'tp'=4] {'req'}, dimensions={0}, use_global_device_ids=true | all-gather | bytes 9216 | tf_op jit(solution)/shard_map/all_gather | solution.py:96
  33.2 0.7 dynamic_slice.18
  33.9 0.8 convolution_convert_fusion.4
  34.8 0.1 reshape_squeeze.12
  34.9 0.1 reshape_squeeze.14
  35.0 1.5 %fusion.51 = (bf16[1,1536,256]{2,1,0:T(8,128)(2,1)S(1)}, bf16[1,1536,256]{2,1,0:T(8,128)(2,1)S(1)}) fusion(bf16[2,1536,256]{2,1,0:T(8,128)(2,1)} %param.18), kind=kLoop, calls=%fused_computation.87 | loop fusion | bytes 3145728 | tf_op jit(solution)/shard_map/slice | solution.py:109
  36.5 1.2 %copy.33 = bf16[1,1536,256]{1,2,0:T(8,128)(2,1)} copy(bf16[1,1536,256]{2,1,0:T(8,128)(2,1)S(1)} %get-tuple-element.139) | data formatting | bytes 1572864
  37.6 1.2 %copy.35 = bf16[1,1536,256]{1,2,0:T(8,128)(2,1)} copy(bf16[1,1536,256]{2,1,0:T(8,128)(2,1)S(1)} %get-tuple-element.140) | data formatting | bytes 1572864
  38.8 1.5 %fusion.52 = (bf16[1,1536,256]{2,1,0:T(8,128)(2,1)S(1)}, bf16[1,1536,256]{2,1,0:T(8,128)(2,1)S(1)}) fusion(bf16[2,1536,256]{2,1,0:T(8,128)(2,1)} %param.19), kind=kLoop, calls=%fused_computation.88 | loop fusion | bytes 3145728 | tf_op jit(solution)/shard_map/slice | solution.py:110
  40.3 0.0 copy-start.4
  40.3 0.3 copy.34
  40.6 0.3 copy.36
  40.9 0.7 iota_compare_fusion.9
  41.6 0.7 iota_compare_fusion.8
  42.3 0.0 copy-done.4
  42.3 10.1 %all-gather.4.cloned.1.call-done = bf16[512,1024]{1,0:T(8,128)(2,1)} async-done(((bf16[64,1024]{1,0:T(8,128)(2,1)}), bf16[512,1024]{1,0:T(8,128)(2,1)}) %all-gather.4.cloned.1.call-update) | async-done | bytes 1048592 | tf_op jit(solution)/shard_map/all_gather | solution.py:92
  52.5 1.5 %convert_reduce_fusion = f32[512]{0:T(512)S(1)} fusion(bf16[512,1024]{1,0:T(8,128)(2,1)} %all-gather.4.cloned.1.call-done), kind=kLoop, calls=%fused_computation.35 | loop fusion | flops 1048064 | bytes 1050624 | tf_op jit(solution)/shard_map/reduce_sum | solution.py:16
  54.0 0.0 copy-done.1
  54.0 0.4 fusion.22
  54.4 0.5 convolution_convert_fusion
  54.9 0.5 copy-done.7
  55.5 0.5 convolution_convert_fusion.1
  56.0 2.4 %while.20 = (s32[]{:T(128)}, f32[4,1536]{1,0:T(4,128)S(1)}, s32[]{:T(128)}, bf16[1536,256]{0,1:T(8,128)(2,1)}, bf16[4,64]{1,0:T(4,128)(2,1)S(1)}, /*index=5*/s32...) while((s32[]{:T(128)}, f32[4,1536]{1,0:T(4,128)S(1)}, ...), condition=%wide.region_4.5_spmd, body=%wide.region_2.4_spmd.sunk | while | flops 269882368 | bytes 1903791 | solution.py:62
  56.0 0.1 subtract_minimum_fusion.4
  56.1 0.5 fusion.97
  56.6 0.1 fusion.98
  56.7 1.5 %multiply_reduce_fusion.5 = (f32[512,4]{0,1:T(4,128)S(1)}, bf16[512,256]{0,1:T(8,128)(2,1)S(1)}) fusion(bf16[1536,256]{0,1:T(8,128)(2,1)} %get-tuple-element.324, s32[]{:T(128)S(6)} %select_n.77, bf16[512,256]{1,0:T(8,128)(2,1)S(1)} %get-tuple-element.328, s32[512]{0:T(512)S(1)} %get-tuple-element.245), kind=kOutput, calls=%fused_computation.4.clone.1 | convolution fusion | flops 134871040 | bytes 796676 | tf_op jit(solution)/shard_map/while/body/dot_general | solution.py:42
  58.2 0.1 fusion.99
  58.4 0.1 select_reduce_fusion.1
  58.5 0.2 fusion.30
  58.7 0.1 fusion.32
  58.8 2.4 %while.21 = (s32[]{:T(128)}, f32[4,1536]{1,0:T(4,128)S(1)}, s32[]{:T(128)}, bf16[1536,256]{0,1:T(8,128)(2,1)}, bf16[4,64]{1,0:T(4,128)(2,1)S(1)}, /*index=5*/s32...) while((s32[]{:T(128)}, f32[4,1536]{1,0:T(4,128)S(1)}, ...), condition=%wide.region_9.10_spmd, body=%wide.region_7.9_spmd.sunk | while | flops 269882368 | bytes 1903791 | solution.py:62
  58.9 0.1 subtract_minimum_fusion.5
  58.9 0.5 fusion.107
  59.4 0.1 fusion.108
  59.6 1.5 %multiply_reduce_fusion.6 = (f32[512,4]{0,1:T(4,128)S(1)}, bf16[512,256]{0,1:T(8,128)(2,1)S(1)}) fusion(bf16[1536,256]{0,1:T(8,128)(2,1)} %get-tuple-element.288, s32[]{:T(128)S(6)} %select_n.78, bf16[512,256]{1,0:T(8,128)(2,1)S(1)} %get-tuple-element.292, s32[512]{0:T(512)S(1)} %get-tuple-element.257), kind=kOutput, calls=%fused_computation.21.clone.1 | convolution fusion | flops 134871040 | bytes 796676 | tf_op jit(solution)/shard_map/while/body/dot_general | solution.py:42
  61.1 0.1 fusion.109
  61.2 0.0 copy-start.2
  61.3 0.0 copy-start.3
  61.3 0.0 copy-start.5
  61.3 0.0 copy-start.6
  61.3 0.1 select_reduce_fusion
  61.4 0.2 fusion.31
  61.6 0.1 fusion.33
  61.7 0.3 fusion.28
  62.0 0.1 convert_element_type.81
  62.1 0.3 fusion.26
  62.4 0.1 convert_element_type.84
  62.6 22.3 %all-gather.1 = bf16[8,2,256]{2,1,0:T(2,128)(2,1)S(1)} all-gather(bf16[1,2,256]{2,1,0:T(2,128)(2,1)S(1)} %maximum_bitcast_fusion), channel_id=1, replica_groups=mesh['req'=8,'tp'=4] {'req'}, dimensions={0}, use_global_device_ids=true | all-gather | bytes 9216 | tf_op jit(solution)/shard_map/all_gather | solution.py:118
  84.9 0.0 copy-done.2
  84.9 0.3 fusion.24
  85.2 5.7 %psum.7 = f32[2,1024]{1,0:T(2,128)S(1)} all-reduce(f32[2,1024]{1,0:T(2,128)S(1)} %fusion.24), channel_id=1, replica_groups=mesh['req'=8,'tp'=4] {'tp'}, use_global_device_ids=true, to_apply=%region_12.13 | all-reduce | flops 2048 | bytes 16384 | tf_op jit(solution)/shard_map/psum | solution.py:128
  91.0 0.0 copy-done.3
  91.0 0.1 fusion.35
  91.1 0.2 multiply_reduce_fusion.2
  91.3 0.0 copy-done.5
  91.3 0.0 copy-done.6
  91.3 0.6 fusion.38
  (18 shorter events, 0.2 us)
Async XLA Ops:
  6.5 3.5 %copy-start = (bf16[1024,256]{1,0:T(8,128)(2,1)S(1)}, bf16[1024,256]{1,0:T(8,128)(2,1)}, u32[]{:S(2)}) copy-start(bf16[1024,256]{1,0:T(8,128)(2,1)} %param.23) | copy-start | bytes 1572868
  6.5 45.9 %all-gather.4.cloned.1.call-start = ((), (), s32[]{:S(2)}) async-start(), calls=%async_computation | async-start | bytes 1179648 | tf_op jit(solution)/shard_map/all_gather | solution.py:92
  40.3 2.0 %copy-start.4 = (s32[2,1536]{1,0:T(2,128)S(1)}, s32[2,1536]{1,0:T(2,128)}, u32[]{:S(2)}) copy-start(s32[2,1536]{1,0:T(2,128)} %param.21) | copy-start | bytes 36868
  52.5 1.5 %copy-start.1 = (bf16[512,1024]{1,0:T(8,128)(2,1)S(1)}, bf16[512,1024]{1,0:T(8,128)(2,1)}, u32[]{:S(2)}) copy-start(bf16[512,1024]{1,0:T(8,128)(2,1)} %all-gather.4.cloned.1.call-done) | copy-start | bytes 3145732
  54.4 1.0 %copy-start.7 = (bf16[1024,256]{1,0:T(8,128)(2,1)S(1)}, bf16[1024,256]{1,0:T(8,128)(2,1)}, u32[]{:S(2)}) copy-start(bf16[1024,256]{1,0:T(8,128)(2,1)} %param.24) | copy-start | bytes 1572868
  61.2 23.7 %copy-start.2 = (bf16[256,1024]{1,0:T(8,128)(2,1)S(1)}, bf16[256,1024]{1,0:T(8,128)(2,1)}, u32[]{:S(2)}) copy-start(bf16[256,1024]{1,0:T(8,128)(2,1)} %param.25) | copy-start | bytes 1572868
  61.3 29.7 %copy-start.3 = (bf16[2,1024]{1,0:T(2,128)(2,1)S(1)}, bf16[2,1024]{1,0:T(2,128)(2,1)}, u32[]{:S(2)}) copy-start(bf16[2,1024]{1,0:T(2,128)(2,1)} %param.16) | copy-start | bytes 12292
  61.3 30.1 %copy-start.5 = (f32[256]{0:T(256)S(1)}, f32[256]{0:T(256)}, u32[]{:S(2)}) copy-start(f32[256]{0:T(256)} %param.27) | copy-start | bytes 3076
  61.3 30.0 %copy-start.6 = (f32[256]{0:T(256)S(1)}, f32[256]{0:T(256)}, u32[]{:S(2)}) copy-start(f32[256]{0:T(256)} %param.26) | copy-start | bytes 3076
Sparse Core Ops, SparseCore 0:
  9.5 42.9 all-gather.3
where the time goes:
time: 99.3 us; the launch traced here: 98.8 us
  blocking collectives  50.3 us (51%)
  between operations  15 us (15%)
  waiting for transfers between devices  10.9 us (11%)
  local copies, waits for them, and re-layouts  8.97 us (9%)
  matrix products  8.17 us (8%)
  other arithmetic  5.37 us (5%)
    all_gather x1, blocking collectives, per_device(): all_contexts = lax.all_gather(own_context, 'req', axis=0, tiled=True)  22.3 us
    all_gather x1, blocking collectives, per_device(): all_queries = lax.all_gather(queries, 'req', axis=0, tiled=True)  22.3 us
    all_gather x1, waiting for transfers between devices, per_device(): lax.all_gather(rel_table, 'req', axis=0, tiled=True)  10.1 us
    psum x1, blocking collectives, per_device(): row_sum = lax.psum(partial_out, 'tp')  5.75 us
    unnamed x22, local copies, waits for them, and re-layouts  3.5 us
    dot_general x2, matrix products, block_scores(): jnp.dot(one_back, rel_query, preferred_element_type=jnp.float32)  2.97 us
  transfers between devices with their start and end apart: 1, of which 1 were waited for; matrix products, arithmetic and copies ran while one was open for 11% of the time, Pallas kernels for 0%

commit v1 on v0

--- a/solution.py
+++ b/solution.py
@@ -125,7 +125,9 @@
     )
     partial_out = jnp.dot(context_rows, w_out, preferred_element_type=jnp.float32)
     col_start = lax.axis_index("tp") * col_width
-    row_sum = lax.psum(partial_out, "tp")
+    row_sum = partial_out
+    for hop in (1, 2):
+        row_sum = row_sum + lax.ppermute(row_sum, "tp", [(dev, dev ^ hop) for dev in range(4)])
     normed_full = norm_rows(row_sum + tokens.astype(jnp.float32))
     own_cols = lax.dynamic_slice_in_dim(normed_full, col_start, col_width, 1)
     return (own_cols * out_gain + out_bias).astype(jnp.bfloat16)

time: 99.3 us -> 98.4 us (level)
  blocking collectives: 50.3 us -> 44.6 us
  waiting for transfers between devices: 10.9 us -> 14.2 us
  starting transfers between devices: 0.01 us -> 1.46 us
    psum x1 -> x0, blocking collectives: 5.75 us -> none  [per_device(): row_sum = lax.psum(partial_out, 'tp')]
    ppermute x0 -> x2, waiting for transfers between devices: none -> 3.38 us  [per_device(): lax.ppermute(row_sum, 'tp', [(dev, dev ^ hop) for dev in range(4)])]
    ppermute x0 -> x2, starting transfers between devices: none -> 1.46 us  [per_device(): lax.ppermute(row_sum, 'tp', [(dev, dev ^ hop) for dev in range(4)])]
  transfers between devices with their start and end apart: 1 -> 3, of which waited for: 1 -> 3; matrix products, arithmetic and copies ran while one was open for 11% -> 12% of each run, Pallas kernels for 0% -> 0%
where the time goes in v1:
time: 98.4 us; the launch traced here: 97.9 us
  blocking collectives  44.6 us (45%)
  between operations  15 us (15%)
  waiting for transfers between devices  14.2 us (14%)
  local copies, waits for them, and re-layouts  8.97 us (9%)
  matrix products  8.17 us (8%)
  other arithmetic  5.37 us (5%)
  starting transfers between devices  1.46 us (1%)
    all_gather x1, blocking collectives, per_device(): all_contexts = lax.all_gather(own_context, 'req', axis=0, tiled=True)  22.3 us
    all_gather x1, blocking collectives, per_device(): all_queries = lax.all_gather(queries, 'req', axis=0, tiled=True)  22.3 us
    all_gather x1, waiting for transfers between devices, per_device(): lax.all_gather(rel_table, 'req', axis=0, tiled=True)  10.1 us
    unnamed x22, local copies, waits for them, and re-layouts  3.5 us
    ppermute x2, waiting for transfers between devices, per_device(): lax.ppermute(row_sum, 'tp', [(dev, dev ^ hop) for dev in range(4)])  3.38 us
    dot_general x2, matrix products, block_scores(): jnp.dot(one_back, rel_query, preferred_element_type=jnp.float32)  2.97 us
  transfers between devices with their start and end apart: 3, of which 3 were waited for; matrix products, arithmetic and copies ran while one was open for 12% of the time, Pallas kernels for 0%

profile of v1, /device:TPU:0, one launch (start us, length us, event | category | flops | bytes accessed | tf_op | source)
XLA Modules:
  0.0 97.9 jit_solution(10320661012566398594)
XLA Ops:
  6.5 0.0 copy-start
  6.5 0.0 all-gather.4.cloned.1.call-start
  6.5 0.7 all-gather.4.cloned.1.call-update
  7.3 1.4 %fusion.51 = (s32[1]{0:T(128)}, s32[1]{0:T(128)}) fusion(s32[2]{0:T(128)} %param.20), kind=kLoop, calls=%fused_computation.89 | loop fusion | bytes 16 | tf_op jit(solution)/shard_map/slice | solution.py:112
  10.1 0.0 copy-done
  10.1 0.9 fusion.25
  10.9 22.3 %all-gather = bf16[8,2,256]{2,1,0:T(2,128)(2,1)S(1)} all-gather(bf16[1,2,256]{2,1,0:T(2,128)(2,1)S(1)} %fusion.25), channel_id=1, replica_groups=mesh['req'=8,'tp'=4] {'req'}, dimensions={0}, use_global_device_ids=true | all-gather | bytes 9216 | tf_op jit(solution)/shard_map/all_gather | solution.py:96
  33.2 0.7 dynamic_slice.18
  33.9 0.8 convolution_convert_fusion.4
  34.8 0.1 reshape_squeeze.12
  34.9 0.1 reshape_squeeze.14
  35.0 1.5 %fusion.49 = (bf16[1,1536,256]{2,1,0:T(8,128)(2,1)S(1)}, bf16[1,1536,256]{2,1,0:T(8,128)(2,1)S(1)}) fusion(bf16[2,1536,256]{2,1,0:T(8,128)(2,1)} %param.18), kind=kLoop, calls=%fused_computation.87 | loop fusion | bytes 3145728 | tf_op jit(solution)/shard_map/slice | solution.py:109
  36.5 1.2 %copy.33 = bf16[1,1536,256]{1,2,0:T(8,128)(2,1)} copy(bf16[1,1536,256]{2,1,0:T(8,128)(2,1)S(1)} %get-tuple-element.139) | data formatting | bytes 1572864
  37.6 1.2 %copy.35 = bf16[1,1536,256]{1,2,0:T(8,128)(2,1)} copy(bf16[1,1536,256]{2,1,0:T(8,128)(2,1)S(1)} %get-tuple-element.140) | data formatting | bytes 1572864
  38.8 1.5 %fusion.50 = (bf16[1,1536,256]{2,1,0:T(8,128)(2,1)S(1)}, bf16[1,1536,256]{2,1,0:T(8,128)(2,1)S(1)}) fusion(bf16[2,1536,256]{2,1,0:T(8,128)(2,1)} %param.19), kind=kLoop, calls=%fused_computation.88 | loop fusion | bytes 3145728 | tf_op jit(solution)/shard_map/slice | solution.py:110
  40.3 0.0 copy-start.4
  40.3 0.3 copy.34
  40.6 0.3 copy.36
  40.9 0.7 iota_compare_fusion.9
  41.6 0.7 iota_compare_fusion.8
  42.3 0.0 copy-done.4
  42.3 10.1 %all-gather.4.cloned.1.call-done = bf16[512,1024]{1,0:T(8,128)(2,1)} async-done(((bf16[64,1024]{1,0:T(8,128)(2,1)}), bf16[512,1024]{1,0:T(8,128)(2,1)}) %all-gather.4.cloned.1.call-update) | async-done | bytes 1048592 | tf_op jit(solution)/shard_map/all_gather | solution.py:92
  52.5 1.5 %convert_reduce_fusion = f32[512]{0:T(512)S(1)} fusion(bf16[512,1024]{1,0:T(8,128)(2,1)} %all-gather.4.cloned.1.call-done), kind=kLoop, calls=%fused_computation.35 | loop fusion | flops 1048064 | bytes 1050624 | tf_op jit(solution)/shard_map/reduce_sum | solution.py:16
  54.0 0.0 copy-done.1
  54.0 0.4 fusion.22
  54.4 0.5 convolution_convert_fusion
  54.9 0.5 copy-done.7
  55.5 0.5 convolution_convert_fusion.1
  56.0 2.4 %while.20 = (s32[]{:T(128)}, f32[4,1536]{1,0:T(4,128)S(1)}, s32[]{:T(128)}, bf16[1536,256]{0,1:T(8,128)(2,1)}, bf16[4,64]{1,0:T(4,128)(2,1)S(1)}, /*index=5*/s32...) while((s32[]{:T(128)}, f32[4,1536]{1,0:T(4,128)S(1)}, ...), condition=%wide.region_4.5_spmd, body=%wide.region_2.4_spmd.sunk | while | flops 269882368 | bytes 1903791 | solution.py:62
  56.0 0.1 subtract_minimum_fusion.4
  56.1 0.5 fusion.95
  56.6 0.1 fusion.96
  56.7 1.5 %multiply_reduce_fusion.5 = (f32[512,4]{0,1:T(4,128)S(1)}, bf16[512,256]{0,1:T(8,128)(2,1)S(1)}) fusion(bf16[1536,256]{0,1:T(8,128)(2,1)} %get-tuple-element.324, s32[]{:T(128)S(6)} %select_n.77, bf16[512,256]{1,0:T(8,128)(2,1)S(1)} %get-tuple-element.328, s32[512]{0:T(512)S(1)} %get-tuple-element.245), kind=kOutput, calls=%fused_computation.4.clone.1 | convolution fusion | flops 134871040 | bytes 796676 | tf_op jit(solution)/shard_map/while/body/dot_general | solution.py:42
  58.2 0.1 fusion.97
  58.4 0.1 select_reduce_fusion.1
  58.5 0.2 fusion.30
  58.7 0.1 fusion.32
  58.8 2.4 %while.21 = (s32[]{:T(128)}, f32[4,1536]{1,0:T(4,128)S(1)}, s32[]{:T(128)}, bf16[1536,256]{0,1:T(8,128)(2,1)}, bf16[4,64]{1,0:T(4,128)(2,1)S(1)}, /*index=5*/s32...) while((s32[]{:T(128)}, f32[4,1536]{1,0:T(4,128)S(1)}, ...), condition=%wide.region_9.10_spmd, body=%wide.region_7.9_spmd.sunk | while | flops 269882368 | bytes 1903791 | solution.py:62
  58.9 0.1 subtract_minimum_fusion.5
  58.9 0.5 fusion.105
  59.4 0.1 fusion.106
  59.6 1.5 %multiply_reduce_fusion.6 = (f32[512,4]{0,1:T(4,128)S(1)}, bf16[512,256]{0,1:T(8,128)(2,1)S(1)}) fusion(bf16[1536,256]{0,1:T(8,128)(2,1)} %get-tuple-element.288, s32[]{:T(128)S(6)} %select_n.78, bf16[512,256]{1,0:T(8,128)(2,1)S(1)} %get-tuple-element.292, s32[512]{0:T(512)S(1)} %get-tuple-element.257), kind=kOutput, calls=%fused_computation.21.clone.1 | convolution fusion | flops 134871040 | bytes 796676 | tf_op jit(solution)/shard_map/while/body/dot_general | solution.py:42
  61.1 0.1 fusion.107
  61.2 0.0 copy-start.2
  61.3 0.0 copy-start.3
  61.3 0.0 copy-start.5
  61.3 0.0 copy-start.6
  61.3 0.1 select_reduce_fusion
  61.4 0.2 fusion.31
  61.6 0.1 fusion.33
  61.7 0.3 fusion.28
  62.0 0.1 convert_element_type.81
  62.1 0.3 fusion.26
  62.4 0.1 convert_element_type.84
  62.6 22.3 %all-gather.1 = bf16[8,2,256]{2,1,0:T(2,128)(2,1)S(1)} all-gather(bf16[1,2,256]{2,1,0:T(2,128)(2,1)S(1)} %maximum_bitcast_fusion), channel_id=1, replica_groups=mesh['req'=8,'tp'=4] {'req'}, dimensions={0}, use_global_device_ids=true | all-gather | bytes 9216 | tf_op jit(solution)/shard_map/all_gather | solution.py:118
  84.9 0.0 copy-done.2
  84.9 0.3 fusion.24
  85.2 0.0 collective-permute-start
  85.2 1.2 %collective-permute-done = f32[2,1024]{1,0:T(2,128)S(1)} collective-permute-done((f32[2,1024]{1,0:T(2,128)S(1)}, f32[2,1024]{1,0:T(2,128)S(1)}, u32[]{:S(2)}, u32[]{:S(2)}) %collective-permute-start) | collective-permute-done | bytes 8224 | tf_op jit(solution)/shard_map/ppermute | solution.py:130
  86.4 1.5 %collective-permute-start.1 = (f32[2,1024]{1,0:T(2,128)S(1)}, f32[2,1024]{1,0:T(2,128)S(1)}, u32[]{:S(2)}, u32[]{:S(2)}) collective-permute-start(f32[2,1024]{1,0:T(2,128)S(1)} %add.95), channel_id=1, source_target_pairs={{0,2},{1,3},{2,0},{3,1},{4,6},{5,7},{6,4},{7,5},{8,10},{9,11},{10,... | collective-permute-start | bytes 24584 | tf_op jit(solution)/shard_map/ppermute | solution.py:130
  87.9 2.2 %collective-permute-done.1 = f32[2,1024]{1,0:T(2,128)S(1)} collective-permute-done((f32[2,1024]{1,0:T(2,128)S(1)}, f32[2,1024]{1,0:T(2,128)S(1)}, u32[]{:S(2)}, u32[]{:S(2)}) %collective-permute-start.1) | collective-permute-done | bytes 8224 | tf_op jit(solution)/shard_map/ppermute | solution.py:130
  90.1 0.1 fusion.46
  90.2 0.2 multiply_reduce_fusion.2
  90.4 0.6 fusion.36
  (22 shorter events, 0.2 us)
Async XLA Ops:
  6.5 3.5 %copy-start = (bf16[1024,256]{1,0:T(8,128)(2,1)S(1)}, bf16[1024,256]{1,0:T(8,128)(2,1)}, u32[]{:S(2)}) copy-start(bf16[1024,256]{1,0:T(8,128)(2,1)} %param.23) | copy-start | bytes 1572868
  6.5 45.9 %all-gather.4.cloned.1.call-start = ((), (), s32[]{:S(2)}) async-start(), calls=%async_computation | async-start | bytes 1179648 | tf_op jit(solution)/shard_map/all_gather | solution.py:92
  40.3 2.0 %copy-start.4 = (s32[2,1536]{1,0:T(2,128)S(1)}, s32[2,1536]{1,0:T(2,128)}, u32[]{:S(2)}) copy-start(s32[2,1536]{1,0:T(2,128)} %param.21) | copy-start | bytes 36868
  52.5 1.5 %copy-start.1 = (bf16[512,1024]{1,0:T(8,128)(2,1)S(1)}, bf16[512,1024]{1,0:T(8,128)(2,1)}, u32[]{:S(2)}) copy-start(bf16[512,1024]{1,0:T(8,128)(2,1)} %all-gather.4.cloned.1.call-done) | copy-start | bytes 3145732
  54.4 1.0 %copy-start.7 = (bf16[1024,256]{1,0:T(8,128)(2,1)S(1)}, bf16[1024,256]{1,0:T(8,128)(2,1)}, u32[]{:S(2)}) copy-start(bf16[1024,256]{1,0:T(8,128)(2,1)} %param.24) | copy-start | bytes 1572868
  61.2 23.7 %copy-start.2 = (bf16[256,1024]{1,0:T(8,128)(2,1)S(1)}, bf16[256,1024]{1,0:T(8,128)(2,1)}, u32[]{:S(2)}) copy-start(bf16[256,1024]{1,0:T(8,128)(2,1)} %param.25) | copy-start | bytes 1572868
  61.3 28.8 %copy-start.3 = (bf16[2,1024]{1,0:T(2,128)(2,1)S(1)}, bf16[2,1024]{1,0:T(2,128)(2,1)}, u32[]{:S(2)}) copy-start(bf16[2,1024]{1,0:T(2,128)(2,1)} %param.16) | copy-start | bytes 12292
  61.3 29.1 %copy-start.5 = (f32[256]{0:T(256)S(1)}, f32[256]{0:T(256)}, u32[]{:S(2)}) copy-start(f32[256]{0:T(256)} %param.27) | copy-start | bytes 3076
  61.3 29.1 %copy-start.6 = (f32[256]{0:T(256)S(1)}, f32[256]{0:T(256)}, u32[]{:S(2)}) copy-start(f32[256]{0:T(256)} %param.26) | copy-start | bytes 3076
  85.2 1.2 %collective-permute-start = (f32[2,1024]{1,0:T(2,128)S(1)}, f32[2,1024]{1,0:T(2,128)S(1)}, u32[]{:S(2)}, u32[]{:S(2)}) collective-permute-start(f32[2,1024]{1,0:T(2,128)S(1)} %fusion.24), channel_id=1, source_target_pairs={{0,1},{1,0},{2,3},{3,2},{4,5},{5,4},{6,7},{7,6},{8,9},{9,8},{10,11... | collective-permute-start | bytes 24584 | tf_op jit(solution)/shard_map/ppermute | solution.py:130
  86.4 3.7 %collective-permute-start.1 = (f32[2,1024]{1,0:T(2,128)S(1)}, f32[2,1024]{1,0:T(2,128)S(1)}, u32[]{:S(2)}, u32[]{:S(2)}) collective-permute-start(f32[2,1024]{1,0:T(2,128)S(1)} %add.95), channel_id=1, source_target_pairs={{0,2},{1,3},{2,0},{3,1},{4,6},{5,7},{6,4},{7,5},{8,10},{9,11},{10,... | collective-permute-start | bytes 24584 | tf_op jit(solution)/shard_map/ppermute | solution.py:130
Sparse Core Ops, SparseCore 0:
  9.5 42.9 all-gather.3
